TPU v7x, 512 devices: a whole 4x4x16 slice. The times are simulated.
512 devices in a mesh: dp: 4 (over y), ctx: 128 (over z, x, core).
Axes of the slice: x: 4, y: 4, z: 16, core: 2. Of those that a mesh axis runs over, the one named last changes fastest.
Arguments:
- queries: bfloat16 [147456, 2048], P(('dp', 'ctx')), may hold values from -6.5 to 6.5
- key_rows: bfloat16 [147456, 512], P(('dp', 'ctx')), may hold values from -6.5 to 6.5
- value_rows: bfloat16 [147456, 512], P(('dp', 'ctx')), may hold values from -6 to 6
- slab_row: int32 [147456], P(('dp', 'ctx')), may hold values from -1 to 131071, as said below
- doc_lengths: int32 [4, 96], P('dp'), may hold values from 1 to 512, 32768 in all within a row
- out_grad: bfloat16 [131072, 2048], P(('dp', 'ctx')), may hold values from -6 to 6
Outputs:
- grad_queries: bfloat16 [131072, 2048], P(('dp', 'ctx'))
- grad_keys: bfloat16 [131072, 512], P(('dp', 'ctx'))
- grad_values: bfloat16 [131072, 512], P(('dp', 'ctx'))
Inputs may be any that keep to these rules, and one draw needn't show every extreme that they name: `slab_row`: every slab row is named by exactly one loader row. The loader rows on device d (in the order dp, ctx) name slab rows of window d // 128 only; each loader device's 288 rows name exactly 256 slab rows; to each block of 256 slab rows that starts at a multiple of 256, one loader device sends either exactly 4 rows or none.
All inputs are finite; a program needn't handle non-finite values.
Results may differ from a plain program's by a relative error of at most 0.025.
Values may be sent and summed in bfloat16 or wider, within the bound.
A program may use at most 64 MiB of HBM per device.

v0:
```python
import functools

import jax
import jax.numpy as jnp
from jax import lax
from jax.experimental import pallas as pl
from jax.experimental.pallas import tpu as pltpu
from jax.sharding import PartitionSpec as P

HEADS = 16
KV_HEADS = 4
HEAD_DIM = 128
TOK = 256
LOAD = 288
LOAD_PAD = 384
PLANE = 8
NZ = 16
SLAB = PLANE * TOK
HALO = 512
MASKED = -1e30
SCALE = HEAD_DIM ** (-0.5)
MESH = pl.DeviceIdType.MESH
BF16 = jnp.bfloat16
F32 = jnp.float32


def dot(a, b, contract=((1,), (0,))):
    return lax.dot_general(a, b, (contract, ((), ())), preferred_element_type=F32)


def kernel(q_ref, k_ref, v_ref, slot_ref, pos_ref, grad_ref, low_ref, dq_ref, dkv_ref,
           xa0, xa12, slots, gslab, onehot, zs, rs, zr, rr, place, kv, acc, dqs, hs, hr, ps, pr,
           outs, sem_as, sem_ar, sem_zs, sem_zr, sem_es, sem_er):
    dp = lax.axis_index("dp")
    me = lax.axis_index("ctx")
    z = me // PLANE
    j = me % PLANE
    x = j // 2
    c = j % 2
    other = j + 1 - 2 * c
    up = (z + 1) % NZ
    down = (z + NZ - 1) % NZ

    xa0[:, LOAD:, :] = jnp.zeros((PLANE, LOAD_PAD - LOAD, 256), BF16)
    xa12[:, LOAD:, :] = jnp.zeros((PLANE, LOAD_PAD - LOAD, 256), BF16)

    barrier = pltpu.get_barrier_semaphore()
    peers = [(z, (j + d) % PLANE) for d in range(1, PLANE)]
    peers += [((z + d) % NZ, j) for d in range(1, NZ)]
    peers += [(up, other), (down, other)]
    for pz, pj in peers:
        pl.semaphore_signal(barrier, inc=1, device_id=(dp, pz * PLANE + pj), device_id_type=MESH)
    pl.semaphore_wait(barrier, len(peers))

    def remote(src, dst, send, recv, pz, pj):
        pltpu.make_async_remote_copy(
            src_ref=src, dst_ref=dst, send_sem=send, recv_sem=recv,
            device_id=(dp, pz * PLANE + pj), device_id_type=MESH).start()

    def local(src, dst, sem):
        pltpu.make_async_copy(src, dst, sem).start()

    def await_bytes(ref, sem):
        pltpu.make_async_copy(ref, ref, sem).wait()

    rows = pl.ds(0, LOAD)

    def kv_dst():
        return xa0.at[j, rows, pl.ds(0, 128)]

    def pos_dst():
        return xa0.at[j, rows, pl.ds(128, 128)]

    def slot_dst():
        return slots.at[j]

    def q_dst():
        return xa12.at[j, rows, :]

    def grad_dst():
        return gslab.at[pl.ds(pl.multiple_of(j * TOK, TOK), TOK), :]

    def kv_column(pj):
        return pl.ds(pl.multiple_of((pj // 2) * 128, 128), 128)

    def wide_column(pj):
        return pl.ds(pl.multiple_of(pj * 256, 128), 256)

    for d in range(1, PLANE):
        pj = (j + d) % PLANE
        remote(slot_ref, slot_dst(), sem_as.at[0], sem_ar.at[0], z, pj)

        @pl.when(pj % 2 == 0)
        def _():
            remote(k_ref.at[:, kv_column(pj)], kv_dst(), sem_as.at[1], sem_ar.at[1], z, pj)

        @pl.when(pj % 2 == 1)
        def _():
            remote(v_ref.at[:, kv_column(pj)], kv_dst(), sem_as.at[1], sem_ar.at[1], z, pj)

        remote(pos_ref, pos_dst(), sem_as.at[2], sem_ar.at[2], z, pj)
    local(slot_ref, slot_dst(), sem_ar.at[0])

    @pl.when(c == 0)
    def _():
        local(k_ref.at[:, kv_column(j)], kv_dst(), sem_ar.at[1])

    @pl.when(c == 1)
    def _():
        local(v_ref.at[:, kv_column(j)], kv_dst(), sem_ar.at[1])

    local(pos_ref, pos_dst(), sem_ar.at[2])
    for d in range(1, PLANE):
        pj = (j + d) % PLANE
        remote(q_ref.at[:, wide_column(pj)], q_dst(), sem_as.at[3], sem_ar.at[3], z, pj)
    local(q_ref.at[:, wide_column(j)], q_dst(), sem_ar.at[3])
    for d in range(1, PLANE):
        pj = (j + d) % PLANE
        remote(grad_ref.at[:, wide_column(pj)], grad_dst(), sem_as.at[4], sem_ar.at[4], z, pj)
    local(grad_ref.at[:, wide_column(j)], grad_dst(), sem_ar.at[4])

    acc[...] = jnp.zeros_like(acc)

    def plane_of(d):
        return (z + ((d + 1) // 2) * (2 * (d % 2) - 1) + NZ) % NZ

    await_bytes(slots, sem_ar.at[0])
    await_bytes(xa0.at[:, rows, pl.ds(0, 128)], sem_ar.at[1])
    await_bytes(xa0.at[:, rows, pl.ds(128, 128)], sem_ar.at[2])

    def pack_first(zp):
        row = lax.broadcasted_iota(jnp.int32, (128, 4 * LOAD_PAD), 0) + zp * 128
        for quad in range(2):
            wanted = jnp.concatenate([slots[quad * 4 + i, 0:1, :] for i in range(4)], axis=1)
            hot = jnp.where(row == wanted, 1.0, 0.0).astype(BF16)
            onehot[zp, quad] = hot
            block = xa0[quad * 4:quad * 4 + 4].reshape(4 * LOAD_PAD, 256)
            packed = dot(hot, block)
            zs[0, zp, :, quad] = packed[:, :128].astype(BF16).reshape(PLANE, 16, 128)
            rs[zp, quad] = jnp.sum(packed[:, 128:].reshape(PLANE, 16, 128), axis=0).astype(BF16)

    @pl.loop(1, NZ)
    def _(d):
        zp = plane_of(d)
        pack_first(zp)
        remote(zs.at[0, zp], zr.at[0, :, :, z], sem_zs.at[0], sem_zr.at[0], zp, j)
        remote(rs.at[zp], rr.at[:, z], sem_zs.at[1], sem_zr.at[1], zp, j)

    pack_first(z)
    local(zs.at[0, z], zr.at[0, :, :, z], sem_zr.at[0])
    local(rs.at[z], rr.at[:, z], sem_zr.at[1])

    await_bytes(xa12.at[:, rows, :], sem_ar.at[3])

    def pack_second(zp):
        for quad in range(2):
            block = xa12[quad * 4:quad * 4 + 4].reshape(4 * LOAD_PAD, 256)
            packed = dot(onehot[zp, quad], block).astype(BF16)
            zs[1, zp, :, quad] = packed[:, :128].reshape(PLANE, 16, 128)
            zs[2, zp, :, quad] = packed[:, 128:].reshape(PLANE, 16, 128)

    @pl.loop(1, NZ)
    def _(d):
        zp = plane_of(d)
        pack_second(zp)
        remote(zs.at[1, zp], zr.at[1, :, :, z], sem_zs.at[2], sem_zr.at[2], zp, j)

    pack_second(z)
    local(zs.at[1, z], zr.at[1, :, :, z], sem_zr.at[2])

    await_bytes(rr, sem_zr.at[1])
    marks = [jnp.transpose(rr[quad].reshape(NZ * 16, 128).astype(F32)) for quad in range(2)]
    spot = lax.broadcasted_iota(jnp.int32, (TOK, 2 * NZ * 16), 0).astype(F32) + 1.0
    for o in range(PLANE):
        mark = jnp.concatenate([marks[0][o:o + 1], marks[1][o:o + 1]], axis=1)
        place[o] = jnp.where(spot == mark, 1.0, 0.0).astype(BF16)

    def settle(chunk, o):
        return dot(place[o], zr[chunk, o].reshape(2 * NZ * 16, 128)).astype(BF16)

    await_bytes(zr.at[0], sem_zr.at[0])

    @pl.loop(0, PLANE)
    def _(o):
        kv[c, pl.ds(pl.multiple_of(HALO + o * TOK, TOK), TOK), :] = settle(0, o)

    own_kv = kv.at[c, pl.ds(HALO, SLAB), :]
    remote(own_kv, own_kv, sem_es.at[0], sem_er.at[0], z, other)
    tail = kv.at[c, pl.ds(SLAB, HALO), :]
    head = kv.at[c, pl.ds(0, HALO), :]
    remote(tail, head, sem_es.at[1], sem_er.at[1], up, j)
    remote(tail, head, sem_es.at[1], sem_er.at[1], up, other)

    for part in range(4):
        pair = pl.ds(2 * part, 2)

        @pl.loop(1, NZ)
        def _(d):
            zp = plane_of(d)
            remote(zs.at[2, zp, pair], zr.at[2, pair, :, z], sem_zs.at[3], sem_zr.at[3 + part], zp, j)

        local(zs.at[2, z, pair], zr.at[2, pair, :, z], sem_zr.at[3 + part])

    await_bytes(own_kv, sem_er.at[0])
    await_bytes(kv.at[:, pl.ds(0, HALO), :], sem_er.at[1])
    await_bytes(gslab, sem_ar.at[4])

    def attend(head_index, b):
        window = pl.ds(pl.multiple_of(b * TOK, TOK), HALO + TOK)
        query = settle(1 + head_index, b)
        grad = gslab[pl.ds(pl.multiple_of(b * TOK, TOK), TOK), head_index * 128:head_index * 128 + 128]
        keys = kv[0, window, :]
        values = kv[1, window, :]
        key_index = lax.broadcasted_iota(jnp.int32, (HALO + TOK, TOK), 0)
        query_index = lax.broadcasted_iota(jnp.int32, (HALO + TOK, TOK), 1)
        allowed = (key_index >= low_ref[b]) & (key_index <= query_index + HALO)
        score = dot(keys, query, ((1,), (1,)))
        score = jnp.where(allowed, score, MASKED)
        top = jnp.max(score, axis=0, keepdims=True)
        weights = jnp.exp((score - top) * SCALE)
        weights = weights * (1.0 / jnp.sum(weights, axis=0, keepdims=True))
        grad_weights = dot(values, grad, ((1,), (1,)))
        row_dot = jnp.sum(weights * grad_weights, axis=0, keepdims=True)
        grad_score = (weights * (grad_weights - row_dot)).astype(BF16)
        acc[1, window, :] += dot(weights.astype(BF16), grad)
        acc[0, window, :] += dot(grad_score, query) * SCALE
        dqs[head_index, b] = (dot(grad_score, keys, ((0,), (0,))) * SCALE).astype(BF16)
        column = pl.ds(pl.multiple_of(j * 256 + head_index * 128, 128), 128)

        @pl.when(b == j)
        def _():
            local(dqs.at[head_index, b], dq_ref.at[:, column], sem_er.at[2])

        @pl.when(b != j)
        def _():
            remote(dqs.at[head_index, b], dq_ref.at[:, column], sem_es.at[2], sem_er.at[2], z, b)

    await_bytes(zr.at[1], sem_zr.at[2])

    @pl.loop(0, PLANE)
    def _(b):
        attend(0, b)

    for part in range(4):
        await_bytes(zr.at[2, pl.ds(2 * part, 2)], sem_zr.at[3 + part])

        @pl.loop(2 * part, 2 * part + 2)
        def _(b):
            attend(1, b)

        if part == 0:
            hs[...] = acc[:, :HALO, :].astype(BF16)
            remote(hs, hr, sem_es.at[3], sem_er.at[3], down, j)

    await_bytes(hr, sem_er.at[3])
    acc[:, SLAB:, :] += hr[...].astype(F32)
    ps[...] = acc[1 - c, HALO:, :].astype(BF16)
    remote(ps, pr, sem_es.at[4], sem_er.at[4], z, other)
    await_bytes(pr, sem_er.at[4])
    outs[...] = (acc[c, HALO:, :] + pr[...].astype(F32)).astype(BF16).reshape(PLANE, TOK, 128)
    column = pl.ds(pl.multiple_of(x * 128, 128), 128)
    for d in range(1, PLANE):
        pj = (j + d) % PLANE
        remote(outs.at[pj], dkv_ref.at[c, :, column], sem_es.at[5], sem_er.at[5], z, pj)
    local(outs.at[j], dkv_ref.at[c, :, column], sem_er.at[5])

    seven = pl.ds(0, PLANE - 1)
    await_bytes(dkv_ref, sem_er.at[5])
    await_bytes(dq_ref, sem_er.at[2])
    await_bytes(slots.at[seven], sem_as.at[0])
    await_bytes(xa0.at[seven, rows, pl.ds(0, 128)], sem_as.at[1])
    await_bytes(xa0.at[seven, rows, pl.ds(128, 128)], sem_as.at[2])
    await_bytes(xa12.at[seven, rows, :], sem_as.at[3])
    await_bytes(gslab.at[pl.ds(0, 7 * TOK), :], sem_as.at[4])
    most = pl.ds(0, NZ - 1)
    await_bytes(zs.at[0, most], sem_zs.at[0])
    await_bytes(rs.at[most], sem_zs.at[1])
    await_bytes(zs.at[1, most], sem_zs.at[2])
    await_bytes(zs.at[2, most], sem_zs.at[3])
    await_bytes(own_kv, sem_es.at[0])
    await_bytes(kv.at[:, pl.ds(0, HALO), :], sem_es.at[1])
    await_bytes(dqs.at[:, seven], sem_es.at[2])
    await_bytes(hs, sem_es.at[3])
    await_bytes(ps, sem_es.at[4])
    await_bytes(outs.at[seven], sem_es.at[5])


def body(queries, key_rows, value_rows, slab_row, doc_lengths, out_grad):
    me = lax.axis_index("ctx")
    z = me // PLANE
    j = me % PLANE
    kept = slab_row >= 0
    owner = jnp.where(kept, slab_row // TOK % (NZ * PLANE), -1)
    order = jnp.arange(LOAD, dtype=jnp.int32)
    earlier = (owner[:, None] == owner[None, :]) & (order[:, None] < order[None, :])
    rank = jnp.sum(earlier.astype(jnp.int32), axis=0)
    slot = jnp.where(kept, owner * 16 + (j % 4) * 4 + rank, -1)
    slot = jnp.pad(slot, (0, LOAD_PAD - LOAD), constant_values=-1)
    slot = jnp.broadcast_to(slot[None, :], (8, LOAD_PAD))
    lane = jnp.arange(128, dtype=jnp.int32)
    mark = jnp.where(kept, slab_row % TOK + 1, 0)
    pos = jnp.where(lane[None, :] == (owner % PLANE)[:, None], mark[:, None], 0).astype(BF16)
    lengths = doc_lengths[0]
    doc_ends = jnp.cumsum(lengths)
    position = z * SLAB + jnp.arange(SLAB, dtype=jnp.int32)
    doc_start = jnp.sum(
        jnp.where(doc_ends[:, None] <= position[None, :], lengths[:, None], 0), axis=0
    ).reshape(PLANE, 1, TOK)
    base = z * SLAB + jnp.arange(PLANE, dtype=jnp.int32) * TOK - HALO
    low = doc_start - base[:, None, None]
    any_spec = pl.BlockSpec(memory_space=pl.ANY)
    vmem_spec = pl.BlockSpec(memory_space=pltpu.VMEM)
    dq, dkv = pl.pallas_call(
        kernel,
        out_shape=(
            jax.ShapeDtypeStruct((TOK, HEADS * HEAD_DIM), BF16),
            jax.ShapeDtypeStruct((2, TOK, KV_HEADS * HEAD_DIM), BF16),
        ),
        in_specs=[any_spec] * 6 + [vmem_spec],
        out_specs=(any_spec, any_spec),
        scratch_shapes=[
            pltpu.VMEM((PLANE, LOAD_PAD, 256), BF16),
            pltpu.VMEM((PLANE, LOAD_PAD, 256), BF16),
            pltpu.VMEM((PLANE, 8, LOAD_PAD), jnp.int32),
            pltpu.VMEM((SLAB, 256), BF16),
            pltpu.VMEM((NZ, 2, 128, 4 * LOAD_PAD), BF16),
            pltpu.VMEM((3, NZ, PLANE, 2, 16, 128), BF16),
            pltpu.VMEM((NZ, 2, 16, 128), BF16),
            pltpu.VMEM((3, PLANE, 2, NZ, 16, 128), BF16),
            pltpu.VMEM((2, NZ, 16, 128), BF16),
            pltpu.VMEM((PLANE, TOK, 2 * NZ * 16), BF16),
            pltpu.VMEM((2, HALO + SLAB, 128), BF16),
            pltpu.VMEM((2, HALO + SLAB, 128), F32),
            pltpu.VMEM((2, PLANE, TOK, 128), BF16),
            pltpu.VMEM((2, HALO, 128), BF16),
            pltpu.VMEM((2, HALO, 128), BF16),
            pltpu.VMEM((SLAB, 128), BF16),
            pltpu.VMEM((SLAB, 128), BF16),
            pltpu.VMEM((PLANE, TOK, 128), BF16),
            pltpu.SemaphoreType.DMA((5,)),
            pltpu.SemaphoreType.DMA((5,)),
            pltpu.SemaphoreType.DMA((4,)),
            pltpu.SemaphoreType.DMA((7,)),
            pltpu.SemaphoreType.DMA((6,)),
            pltpu.SemaphoreType.DMA((6,)),
        ],
        compiler_params=pltpu.CompilerParams(
            collective_id=0, has_side_effects=True, vmem_limit_bytes=60 * 1024 * 1024
        ),
        name="packed_attention",
    )(queries, key_rows, value_rows, slot, pos, out_grad, low)
    return (dq, dkv[0], dkv[1])


def solution(mesh):
    in_specs = (
        P(("dp", "ctx"), None),
        P(("dp", "ctx"), None),
        P(("dp", "ctx"), None),
        P(("dp", "ctx")),
        P("dp", None),
        P(("dp", "ctx"), None),
    )
    out_specs = (P(("dp", "ctx"), None), P(("dp", "ctx"), None), P(("dp", "ctx"), None))
    return jax.shard_map(body, mesh=mesh, in_specs=in_specs, out_specs=out_specs, check_vma=False)
```

profile of v0, /device:TPU:1, one launch (start us, length us, event | category | flops | bytes accessed | tf_op | source)
XLA Modules:
  0.0 199.7 jit_solution(13537928276969454335)
XLA Ops:
  0.7 0.7 add_select_fusion.1
  1.4 0.1 convert_reduce_fusion
  1.5 0.7 fusion.5
  2.2 0.6 broadcast_in_dim.46.slot_ref
  2.8 0.8 copy.11
  3.6 0.1 reduce-window.8
  3.7 0.1 reduce
  3.8 0.8 select_reduce_fusion
  4.7 0.7 broadcast_subtract_fusion.low_ref
  5.3 0.8 select_convert_fusion.pos_ref
  6.1 190.6 %packed_attention.1 = (bf16[256,2048]{1,0:T(8,128)(2,1)}, bf16[2,256,512]{2,1,0:T(8,128)(2,1)}) custom-call(bf16[288,2048]{1,0:T(8,128)(2,1)} %q_ref.1, bf16[288,512]{1,0:T(8,128)(2,1)} %k_ref.1, bf16[288,512]{1,0:T(8,128)(2,1)} %v_ref.1, s32[8,384]{1,0:T(8,128)} %broadcast_in_dim.46.slot_ref, bf16[288,128]{1,0:T(8,128)(2,1)} %select_convert_fusion.pos_ref, ...), custom_call_target="tpu_custom_call" | custom-call | tf_op jit(solution)/shard_map/packed_attention/pallas_call | solution.py:313
  196.8 0.0 copy-start
  196.8 1.9 slice_bitcast_fusion
  198.7 0.0 copy-done
  198.7 1.0 copy.13
  (3 shorter events, 0.0 us)
Async XLA Ops:
  196.8 2.0 copy-start
where the time goes:
time: 200 us
  Pallas kernels  191 us (96%)
  local copies, waits for them, and re-layouts  4.27 us (2%)
  other arithmetic  4.05 us (2%)
    pallas_call x1, Pallas kernels, body(): pl.pallas_call(kernel, out_shape=(jax.ShapeDtypeStruct((TOK, HEADS * HEAD...  191 us

commit v1 on v0

v1 whole, which is shorter than its diff:
```python
import functools

import jax
import jax.numpy as jnp
from jax import lax
from jax.experimental import pallas as pl
from jax.experimental.pallas import tpu as pltpu
from jax.sharding import PartitionSpec as P

HEADS = 16
KV_HEADS = 4
HEAD_DIM = 128
TOK = 256
LOAD = 288
LOAD_PAD = 384
PLANE = 8
NZ = 16
SLAB = PLANE * TOK
HALO = 512
DOCS = 96
MASKED = -1e30
SCALE = HEAD_DIM ** (-0.5)
MESH = pl.DeviceIdType.MESH
BF16 = jnp.bfloat16
F32 = jnp.float32


def dot(a, b, contract=((1,), (0,))):
    return lax.dot_general(a, b, (contract, ((), ())), preferred_element_type=F32)


def kernel(q_ref, k_ref, v_ref, grad_ref, slab_ref, len_ref, dq_ref, dk_ref, dv_ref,
           slot_out, pos_out, low, xk, xq, slots, gslab, onehot, zs, rs, zr, rr, place, kv, acc,
           dqs, hs, hr, ps, pr, outs, sem_as, sem_ar, sem_zs, sem_zr, sem_es, sem_er, sem_pr):
    dp = lax.axis_index("dp")
    me = lax.axis_index("ctx")
    z = me // PLANE
    j = me % PLANE
    x = j // 2
    c = j % 2
    other = j + 1 - 2 * c
    up = (z + 1) % NZ
    down = (z + NZ - 1) % NZ

    barrier = pltpu.get_barrier_semaphore()
    peers = [(z, (j + d) % PLANE) for d in range(1, PLANE)]
    peers += [((z + d) % NZ, j) for d in range(1, NZ)]
    peers += [(up, other), (down, other)]
    for pz, pj in peers:
        pl.semaphore_signal(barrier, inc=1, device_id=(dp, pz * PLANE + pj), device_id_type=MESH)

    xk[:, LOAD:, :] = jnp.zeros((PLANE, LOAD_PAD - LOAD, 128), BF16)
    xq[:, LOAD:, :] = jnp.zeros((PLANE, LOAD_PAD - LOAD, 384), BF16)
    slab = slab_ref[0:1, :]
    kept = slab >= 0
    owner = jnp.where(kept, (slab >> 8) & (NZ * PLANE - 1), -1)
    owner_f = owner.astype(F32)
    seat_f = jnp.where(kept, owner & (PLANE - 1), -1).astype(F32)
    mark_f = jnp.where(kept, (slab & (TOK - 1)) + 1, 0).astype(F32)
    lane = lax.broadcasted_iota(jnp.int32, (128, LOAD_PAD), 1)
    line = lax.broadcasted_iota(jnp.int32, (128, LOAD_PAD), 0)
    rank = jnp.zeros((1, LOAD_PAD), F32)
    seat_lane = lax.broadcasted_iota(jnp.int32, (128, 128), 1).astype(F32)
    for k in range(3):
        tile = slice(128 * k, 128 * k + 128)
        owner_col = jnp.transpose(jnp.broadcast_to(owner_f[:, tile], (LOAD_PAD, 128)))
        before = (owner_col == owner_f) & (line + 128 * k < lane)
        rank = rank + jnp.sum(jnp.where(before, 1.0, 0.0), axis=0, keepdims=True)
        seat_col = jnp.transpose(jnp.broadcast_to(seat_f[:, tile], (128, 128)))
        mark_col = jnp.transpose(jnp.broadcast_to(mark_f[:, tile], (128, 128)))
        count = min(128, LOAD - 128 * k)
        pos = jnp.where(seat_lane == seat_col, mark_col, 0.0).astype(BF16)
        pos_out[128 * k:128 * k + count, :] = pos[:count]
    slot = jnp.where(kept, owner * 16 + (j % 4) * 4 + rank.astype(jnp.int32), -1)
    slot_out[...] = jnp.broadcast_to(slot, (8, LOAD_PAD))

    pl.semaphore_wait(barrier, len(peers))

    def remote(src, dst, send, recv, pz, pj):
        pltpu.make_async_remote_copy(
            src_ref=src, dst_ref=dst, send_sem=send, recv_sem=recv,
            device_id=(dp, pz * PLANE + pj), device_id_type=MESH).start()

    def local(src, dst, sem):
        pltpu.make_async_copy(src, dst, sem).start()

    def await_bytes(ref, sem):
        pltpu.make_async_copy(ref, ref, sem).wait()

    rows = pl.ds(0, LOAD)
    q_lanes = pl.ds(0, 256)
    pos_lanes = pl.ds(256, 128)

    def kv_dst():
        return xk.at[j, rows, :]

    def pos_dst():
        return xq.at[j, rows, pos_lanes]

    def q_dst():
        return xq.at[j, rows, q_lanes]

    def grad_dst():
        return gslab.at[pl.ds(pl.multiple_of(j * TOK, TOK), TOK), :]

    def kv_column(pj):
        return pl.ds(pl.multiple_of((pj // 2) * 128, 128), 128)

    def wide_column(pj):
        return pl.ds(pl.multiple_of(pj * 256, 128), 256)

    for d in range(1, PLANE):
        pj = (j + d) % PLANE

        @pl.when(pj % 2 == 0)
        def _():
            remote(k_ref.at[:, kv_column(pj)], kv_dst(), sem_as.at[1], sem_ar.at[1], z, pj)

        @pl.when(pj % 2 == 1)
        def _():
            remote(v_ref.at[:, kv_column(pj)], kv_dst(), sem_as.at[1], sem_ar.at[1], z, pj)

        remote(slot_out, slots.at[j], sem_as.at[0], sem_ar.at[0], z, pj)

    local(slot_out, slots.at[j], sem_ar.at[0])

    @pl.when(c == 0)
    def _():
        local(k_ref.at[:, kv_column(j)], kv_dst(), sem_ar.at[1])

    @pl.when(c == 1)
    def _():
        local(v_ref.at[:, kv_column(j)], kv_dst(), sem_ar.at[1])

    for d in range(1, PLANE):
        pj = (j + d) % PLANE
        remote(pos_out, pos_dst(), sem_as.at[2], sem_ar.at[2], z, pj)
        remote(q_ref.at[:, wide_column(pj)], q_dst(), sem_as.at[3], sem_ar.at[3], z, pj)
    local(pos_out, pos_dst(), sem_ar.at[2])
    local(q_ref.at[:, wide_column(j)], q_dst(), sem_ar.at[3])
    for d in range(1, PLANE):
        pj = (j + d) % PLANE
        remote(grad_ref.at[:, wide_column(pj)], grad_dst(), sem_as.at[4], sem_ar.at[4], z, pj)
    local(grad_ref.at[:, wide_column(j)], grad_dst(), sem_ar.at[4])

    def plane_of(d):
        return (z + ((d + 1) // 2) * (2 * (d % 2) - 1) + NZ) % NZ

    await_bytes(slots, sem_ar.at[0])
    await_bytes(xk.at[:, rows, :], sem_ar.at[1])

    def pack_first(zp):
        row = lax.broadcasted_iota(jnp.int32, (128, 4 * LOAD_PAD), 0) + zp * 128
        for quad in range(2):
            wanted = jnp.concatenate([slots[quad * 4 + i, 0:1, :] for i in range(4)], axis=1)
            hot = jnp.where(row == wanted, 1.0, 0.0).astype(BF16)
            onehot[zp, quad] = hot
            block = xk[quad * 4:quad * 4 + 4].reshape(4 * LOAD_PAD, 128)
            zs[0, zp, :, quad] = dot(hot, block).astype(BF16).reshape(PLANE, 16, 128)

    @pl.loop(1, NZ)
    def _(d):
        zp = plane_of(d)
        pack_first(zp)
        remote(zs.at[0, zp], zr.at[0, :, :, z], sem_zs.at[0], sem_zr.at[0], zp, j)

    pack_first(z)
    local(zs.at[0, z], zr.at[0, :, :, z], sem_zr.at[0])

    lengths = jnp.broadcast_to(len_ref[...].astype(F32), (DOCS, DOCS))
    doc_row = lax.broadcasted_iota(jnp.int32, (DOCS, DOCS), 0)
    doc_col = lax.broadcasted_iota(jnp.int32, (DOCS, DOCS), 1)
    doc_ends = jnp.sum(jnp.where(doc_col <= doc_row, lengths, 0.0), axis=1, keepdims=True)
    doc_size = jnp.sum(jnp.where(doc_col == doc_row, lengths, 0.0), axis=1, keepdims=True)
    offset = lax.broadcasted_iota(jnp.int32, (1, TOK), 1)
    for b in range(PLANE):
        place_at = (offset + (z * SLAB + b * TOK)).astype(F32)
        start = jnp.sum(jnp.where(doc_ends <= place_at, doc_size, 0.0), axis=0, keepdims=True)
        low[b] = start.astype(jnp.int32) - (z * SLAB + b * TOK - HALO)
    acc[...] = jnp.zeros_like(acc)

    await_bytes(xq.at[:, rows, pos_lanes], sem_ar.at[2])
    await_bytes(xq.at[:, rows, q_lanes], sem_ar.at[3])

    @pl.loop(0, NZ)
    def _(d):
        zp = plane_of(d)
        for quad in range(2):
            block = xq[quad * 4:quad * 4 + 4].reshape(4 * LOAD_PAD, 384)
            packed = dot(onehot[zp, quad], block)
            zs[1, zp, :, quad] = packed[:, :128].astype(BF16).reshape(PLANE, 16, 128)
            zs[2, zp, :, quad] = packed[:, 128:256].astype(BF16).reshape(PLANE, 16, 128)
            rs[zp, quad] = jnp.sum(packed[:, 256:].reshape(PLANE, 16, 128), axis=0).astype(BF16)

    for d in range(1, NZ):
        zp = plane_of(d)
        remote(rs.at[zp], rr.at[:, z], sem_zs.at[1], sem_zr.at[1], zp, j)
    local(rs.at[z], rr.at[:, z], sem_zr.at[1])
    for d in range(1, NZ):
        zp = plane_of(d)
        remote(zs.at[1, zp], zr.at[1, :, :, z], sem_zs.at[2], sem_zr.at[2], zp, j)
    local(zs.at[1, z], zr.at[1, :, :, z], sem_zr.at[2])

    await_bytes(rr, sem_zr.at[1])
    marks = [jnp.transpose(rr[quad].reshape(NZ * 16, 128).astype(F32)) for quad in range(2)]
    spot = lax.broadcasted_iota(jnp.int32, (TOK, 2 * NZ * 16), 0).astype(F32) + 1.0
    for o in range(PLANE):
        mark = jnp.concatenate([marks[0][o:o + 1], marks[1][o:o + 1]], axis=1)
        place[o] = jnp.where(spot == mark, 1.0, 0.0).astype(BF16)

    def settle(chunk, o):
        return dot(place[o], zr[chunk, o].reshape(2 * NZ * 16, 128)).astype(BF16)

    await_bytes(zr.at[0], sem_zr.at[0])

    @pl.loop(0, PLANE)
    def _(o):
        kv[c, pl.ds(pl.multiple_of(HALO + o * TOK, TOK), TOK), :] = settle(0, o)

    own_kv = kv.at[c, pl.ds(HALO, SLAB), :]
    remote(own_kv, own_kv, sem_es.at[0], sem_er.at[0], z, other)
    tail = kv.at[c, pl.ds(SLAB, HALO), :]
    head = kv.at[c, pl.ds(0, HALO), :]
    remote(tail, head, sem_es.at[1], sem_er.at[1], up, j)
    remote(tail, head, sem_es.at[1], sem_er.at[1], up, other)

    @pl.loop(0, PLANE)
    def _(o):
        @pl.loop(1, NZ)
        def _(d):
            zp = plane_of(d)
            remote(zs.at[2, zp, o], zr.at[2, o, :, z], sem_zs.at[3], sem_zr.at[3 + o], zp, j)

        local(zs.at[2, z, o], zr.at[2, o, :, z], sem_zr.at[3 + o])

    await_bytes(own_kv, sem_er.at[0])
    await_bytes(kv.at[:, pl.ds(0, HALO), :], sem_er.at[1])
    await_bytes(gslab, sem_ar.at[4])

    def attend(head_index, b):
        start = b * TOK if isinstance(b, int) else pl.multiple_of(b * TOK, TOK)
        window = pl.ds(start, HALO + TOK)
        query = settle(1 + head_index, b)
        grad = gslab[pl.ds(start, TOK), head_index * 128:head_index * 128 + 128]
        keys = kv[0, window, :]
        values = kv[1, window, :]
        key_index = lax.broadcasted_iota(jnp.int32, (HALO + TOK, TOK), 0)
        query_index = lax.broadcasted_iota(jnp.int32, (HALO + TOK, TOK), 1)
        allowed = (key_index >= low[b]) & (key_index <= query_index + HALO)
        score = dot(keys, query, ((1,), (1,)))
        score = jnp.where(allowed, score, MASKED)
        top = jnp.max(score, axis=0, keepdims=True)
        weights = jnp.exp((score - top) * SCALE)
        weights = weights * (1.0 / jnp.sum(weights, axis=0, keepdims=True))
        grad_weights = dot(values, grad, ((1,), (1,)))
        row_dot = jnp.sum(weights * grad_weights, axis=0, keepdims=True)
        grad_score = (weights * (grad_weights - row_dot)).astype(BF16)
        acc[1, window, :] += dot(weights.astype(BF16), grad)
        acc[0, window, :] += dot(grad_score, query) * SCALE
        dqs[head_index, b] = (dot(grad_score, keys, ((0,), (0,))) * SCALE).astype(BF16)
        column = pl.ds(pl.multiple_of(j * 256 + head_index * 128, 128), 128)

        @pl.when(j == b)
        def _():
            local(dqs.at[head_index, b], dq_ref.at[:, column], sem_er.at[2])

        @pl.when(j != b)
        def _():
            remote(dqs.at[head_index, b], dq_ref.at[:, column], sem_es.at[2], sem_er.at[2], z, b)

    def hand_over(t):
        ps[t] = acc[1 - c, HALO + t * TOK:HALO + t * TOK + TOK, :].astype(BF16)
        remote(ps.at[t], pr.at[t], sem_es.at[4], sem_pr.at[t], z, other)

    def finish(t):
        await_bytes(pr.at[t], sem_pr.at[t])
        total = acc[c, HALO + t * TOK:HALO + t * TOK + TOK, :] + pr[t].astype(F32)
        outs[t] = total.astype(BF16)
        column = pl.ds(pl.multiple_of(x * 128, 128), 128)
        for which, ref in ((0, dk_ref), (1, dv_ref)):
            @pl.when((c == which) & (j == t))
            def _():
                local(outs.at[t], ref.at[:, column], sem_er.at[4 + which])

            @pl.when((c == which) & (j != t))
            def _():
                remote(outs.at[t], ref.at[:, column], sem_es.at[5], sem_er.at[4 + which], z, t)

    await_bytes(zr.at[1], sem_zr.at[2])

    @pl.loop(0, PLANE)
    def _(b):
        attend(0, b)

    for b in range(PLANE):
        if b == PLANE - 1:
            await_bytes(hr, sem_er.at[3])
            acc[:, SLAB:, :] += hr[...].astype(F32)
        await_bytes(zr.at[2, b], sem_zr.at[3 + b])
        attend(1, b)
        if b == 1:
            hs[...] = acc[:, :HALO, :].astype(BF16)
            remote(hs, hr, sem_es.at[3], sem_er.at[3], down, j)
        if b >= 2:
            hand_over(b - 2)
        if b >= 3:
            finish(b - 3)
    hand_over(6)
    hand_over(7)
    for t in (5, 6, 7):
        finish(t)

    seven = pl.ds(0, PLANE - 1)
    most = pl.ds(0, NZ - 1)
    await_bytes(slots.at[seven], sem_as.at[0])
    await_bytes(xk.at[seven, rows, :], sem_as.at[1])
    await_bytes(xq.at[seven, rows, pos_lanes], sem_as.at[2])
    await_bytes(xq.at[seven, rows, q_lanes], sem_as.at[3])
    await_bytes(gslab.at[pl.ds(0, 7 * TOK), :], sem_as.at[4])
    await_bytes(zs.at[0, most], sem_zs.at[0])
    await_bytes(rs.at[most], sem_zs.at[1])
    await_bytes(zs.at[1, most], sem_zs.at[2])
    await_bytes(zs.at[2, most], sem_zs.at[3])
    await_bytes(own_kv, sem_es.at[0])
    await_bytes(kv.at[:, pl.ds(0, HALO), :], sem_es.at[1])
    await_bytes(dqs.at[:, seven], sem_es.at[2])
    await_bytes(hs, sem_es.at[3])
    await_bytes(ps, sem_es.at[4])
    await_bytes(outs.at[seven], sem_es.at[5])
    await_bytes(dq_ref, sem_er.at[2])
    await_bytes(dk_ref, sem_er.at[4])
    await_bytes(dv_ref, sem_er.at[5])


def body(queries, key_rows, value_rows, slab_row, doc_lengths, out_grad):
    slab = jnp.pad(slab_row, (0, LOAD_PAD - LOAD), constant_values=-1)
    slab = jnp.broadcast_to(slab[None, :], (8, LOAD_PAD))
    any_spec = pl.BlockSpec(memory_space=pl.ANY)
    vmem_spec = pl.BlockSpec(memory_space=pltpu.VMEM)
    return pl.pallas_call(
        kernel,
        out_shape=(
            jax.ShapeDtypeStruct((TOK, HEADS * HEAD_DIM), BF16),
            jax.ShapeDtypeStruct((TOK, KV_HEADS * HEAD_DIM), BF16),
            jax.ShapeDtypeStruct((TOK, KV_HEADS * HEAD_DIM), BF16),
        ),
        in_specs=[any_spec] * 4 + [vmem_spec] * 2,
        out_specs=(any_spec, any_spec, any_spec),
        scratch_shapes=[
            pltpu.VMEM((8, LOAD_PAD), jnp.int32),
            pltpu.VMEM((LOAD, 128), BF16),
            pltpu.VMEM((PLANE, 1, TOK), jnp.int32),
            pltpu.VMEM((PLANE, LOAD_PAD, 128), BF16),
            pltpu.VMEM((PLANE, LOAD_PAD, 384), BF16),
            pltpu.VMEM((PLANE, 8, LOAD_PAD), jnp.int32),
            pltpu.VMEM((SLAB, 256), BF16),
            pltpu.VMEM((NZ, 2, 128, 4 * LOAD_PAD), BF16),
            pltpu.VMEM((3, NZ, PLANE, 2, 16, 128), BF16),
            pltpu.VMEM((NZ, 2, 16, 128), BF16),
            pltpu.VMEM((3, PLANE, 2, NZ, 16, 128), BF16),
            pltpu.VMEM((2, NZ, 16, 128), BF16),
            pltpu.VMEM((PLANE, TOK, 2 * NZ * 16), BF16),
            pltpu.VMEM((2, HALO + SLAB, 128), BF16),
            pltpu.VMEM((2, HALO + SLAB, 128), F32),
            pltpu.VMEM((2, PLANE, TOK, 128), BF16),
            pltpu.VMEM((2, HALO, 128), BF16),
            pltpu.VMEM((2, HALO, 128), BF16),
            pltpu.VMEM((PLANE, TOK, 128), BF16),
            pltpu.VMEM((PLANE, TOK, 128), BF16),
            pltpu.VMEM((PLANE, TOK, 128), BF16),
            pltpu.SemaphoreType.DMA((5,)),
            pltpu.SemaphoreType.DMA((5,)),
            pltpu.SemaphoreType.DMA((4,)),
            pltpu.SemaphoreType.DMA((11,)),
            pltpu.SemaphoreType.DMA((6,)),
            pltpu.SemaphoreType.DMA((6,)),
            pltpu.SemaphoreType.DMA((8,)),
        ],
        compiler_params=pltpu.CompilerParams(
            collective_id=0, has_side_effects=True, vmem_limit_bytes=60 * 1024 * 1024
        ),
        name="packed_attention",
    )(queries, key_rows, value_rows, out_grad, slab, doc_lengths)


def solution(mesh):
    in_specs = (
        P(("dp", "ctx"), None),
        P(("dp", "ctx"), None),
        P(("dp", "ctx"), None),
        P(("dp", "ctx")),
        P("dp", None),
        P(("dp", "ctx"), None),
    )
    out_specs = (P(("dp", "ctx"), None), P(("dp", "ctx"), None), P(("dp", "ctx"), None))
    return jax.shard_map(body, mesh=mesh, in_specs=in_specs, out_specs=out_specs, check_vma=False)
```

time: 200 us -> 191 us (0.955)
  Pallas kernels: 191 us -> 185 us
  other arithmetic: 4.05 us -> 0 us
    pallas_call x1, Pallas kernels: 191 us -> 185 us  [body(): pl.pallas_call(kernel, out_shape=(jax.ShapeDtypeStruct((TOK, HEADS * HEAD...]
    unnamed x3 -> x7, local copies, waits for them, and re-layouts: 0.97 us -> 3.77 us
where the time goes in v1:
time: 191 us
  Pallas kernels  185 us (97%)
  local copies, waits for them, and re-layouts  5.06 us (3%)
    pallas_call x1, Pallas kernels, body(): pl.pallas_call(kernel, out_shape=(jax.ShapeDtypeStruct((TOK, HEADS * HEAD...  185 us

profile of v1, /device:TPU:1, one launch (start us, length us, event | category | flops | bytes accessed | tf_op | source)
XLA Modules:
  0.0 190.9 jit_solution(1832102255862337025)
XLA Ops:
  0.6 0.7 pad.4
  1.3 0.6 broadcast_in_dim.2.slab_ref
  1.9 185.2 %packed_attention.1 = (bf16[256,2048]{1,0:T(8,128)(2,1)}, bf16[256,512]{1,0:T(8,128)(2,1)}, bf16[256,512]{1,0:T(8,128)(2,1)}) custom-call(bf16[288,2048]{1,0:T(8,128)(2,1)} %q_ref.1, bf16[288,512]{1,0:T(8,128)(2,1)} %k_ref.1, bf16[288,512]{1,0:T(8,128)(2,1)} %v_ref.1, bf16[256,2048]{1,0:T(8,128)(2,1)} %grad_ref.1, s32[8,384]{1,0:T(8,128)} %broadcast_in_dim.2.slab_ref, ...), custom_call_target="tpu_custom_call" | custom-call | tf_op jit(solution)/shard_map/packed_attention/pallas_call | solution.py:340
  187.1 0.0 copy-start.1
  187.1 0.0 copy-start
  187.1 2.4 %copy.12 = bf16[256,2048]{1,0:T(8,128)(2,1)} copy(bf16[256,2048]{1,0:T(8,128)(2,1)} %get-tuple-element.6) | data formatting | bytes 2097152
  189.5 0.0 copy-done.1
  189.5 0.7 copy.13
  190.2 0.0 copy-done
  190.2 0.7 copy.14
Async XLA Ops:
  187.1 2.4 %copy-start.1 = (bf16[256,512]{1,0:T(8,128)(2,1)S(1)}, bf16[256,512]{1,0:T(8,128)(2,1)}, u32[]{:S(2)}) copy-start(bf16[256,512]{1,0:T(8,128)(2,1)} %get-tuple-element.7) | copy-start | bytes 786436
  187.1 3.1 %copy-start = (bf16[256,512]{1,0:T(8,128)(2,1)S(1)}, bf16[256,512]{1,0:T(8,128)(2,1)}, u32[]{:S(2)}) copy-start(bf16[256,512]{1,0:T(8,128)(2,1)} %get-tuple-element.8) | copy-start | bytes 786436

commit v2 on v0

--- a/solution.py
+++ b/solution.py
@@ -17,6 +17,9 @@
 NZ = 16
 SLAB = PLANE * TOK
 HALO = 512
+DOCS = 96
+NDP = 4
+CAP = 176
 MASKED = -1e30
 SCALE = HEAD_DIM ** (-0.5)
 MESH = pl.DeviceIdType.MESH
@@ -28,7 +31,7 @@
     return lax.dot_general(a, b, (contract, ((), ())), preferred_element_type=F32)
 
 
-def kernel(q_ref, k_ref, v_ref, slot_ref, pos_ref, grad_ref, low_ref, dq_ref, dkv_ref,
+def spread_kernel(q_ref, k_ref, v_ref, slot_ref, pos_ref, grad_ref, low_ref, dq_ref, dkv_ref,
            xa0, xa12, slots, gslab, onehot, zs, rs, zr, rr, place, kv, acc, dqs, hs, hr, ps, pr,
            outs, sem_as, sem_ar, sem_zs, sem_zr, sem_es, sem_er):
     dp = lax.axis_index("dp")
@@ -285,7 +288,446 @@
     await_bytes(outs.at[seven], sem_es.at[5])
 
 
-def body(queries, key_rows, value_rows, slab_row, doc_lengths, out_grad):
+def mixed_kernel(q_ref, k_ref, v_ref, grad_ref, slab_ref, len_ref, dq_ref, dk_ref, dv_ref, flag_ref,
+                 low, raw_kv, raw_q, sort_kv, sort_q, meta_out, meta_in, xk, xq, srow, info, gslab,
+                 onehot, zs, ms, zr, mr, drow, spread, whole, ys, yr, ym_out, ym_in, place, kv, acc,
+                 dqs, hs, hr, ps, pr, outs, sem_in, sem_as, sem_ar, sem_zs, sem_zr, sem_ys, sem_yr,
+                 sem_es, sem_er, sem_pr):
+    dp = lax.axis_index("dp")
+    me = lax.axis_index("ctx")
+    z = me // PLANE
+    j = me % PLANE
+    x = j // 2
+    c = j % 2
+    other = j + 1 - 2 * c
+    up = (z + 1) % NZ
+    down = (z + NZ - 1) % NZ
+
+    barrier = pltpu.get_barrier_semaphore()
+    plane = [((dp + e) % NDP, (j + d) % PLANE) for e in range(NDP) for d in range(PLANE)]
+    peers = [(py, z, pj) for py, pj in plane[1:]]
+    peers += [(dp, (z + d) % NZ, j) for d in range(1, NZ)]
+    peers += [(dp, up, other), (dp, down, other)]
+    for py, pz, pj in peers:
+        pl.semaphore_signal(barrier, inc=1, device_id=(py, pz * PLANE + pj), device_id_type=MESH)
+
+    def remote(src, dst, send, recv, pz, pj, py=dp):
+        pltpu.make_async_remote_copy(
+            src_ref=src, dst_ref=dst, send_sem=send, recv_sem=recv,
+            device_id=(py, pz * PLANE + pj), device_id_type=MESH).start()
+
+    def local(src, dst, sem):
+        pltpu.make_async_copy(src, dst, sem).start()
+
+    def await_bytes(ref, sem):
+        pltpu.make_async_copy(ref, ref, sem).wait()
+
+    rows = pl.ds(0, LOAD)
+    key_lanes = pl.ds(0, 512)
+    value_lanes = pl.ds(512, 512)
+    local(k_ref, raw_kv.at[rows, key_lanes], sem_in.at[0])
+    local(v_ref, raw_kv.at[rows, value_lanes], sem_in.at[1])
+    local(q_ref, raw_q.at[rows, :], sem_in.at[2])
+
+    raw_kv[LOAD:, :] = jnp.zeros((LOAD_PAD - LOAD, 1024), BF16)
+    raw_q[LOAD:, :] = jnp.zeros((LOAD_PAD - LOAD, 2048), BF16)
+    slab = slab_ref[0:1, :]
+    kept = slab >= 0
+    owner_f = jnp.where(kept, (slab >> 8) & (NZ * PLANE - 1), -1).astype(F32)
+    mark_f = jnp.where(kept, (slab & (TOK - 1)) + 1, 0).astype(F32)
+    lane = lax.broadcasted_iota(jnp.int32, (128, LOAD_PAD), 1)
+    line = lax.broadcasted_iota(jnp.int32, (128, LOAD_PAD), 0)
+    rank = jnp.zeros((1, LOAD_PAD), F32)
+    less = jnp.zeros((1, LOAD_PAD), F32)
+    for k in range(3):
+        tile = slice(128 * k, 128 * k + 128)
+        owner_col = jnp.transpose(jnp.broadcast_to(owner_f[:, tile], (LOAD_PAD, 128)))
+        same = (owner_col == owner_f) & (line + 128 * k < lane)
+        under = (owner_col < owner_f) & (owner_col >= 0.0)
+        rank = rank + jnp.sum(jnp.where(same, 1.0, 0.0), axis=0, keepdims=True)
+        less = less + jnp.sum(jnp.where(under, 1.0, 0.0), axis=0, keepdims=True)
+    seat = jnp.where(kept, rank * 64.0 + less * 0.25, -1.0)
+    line_f = line.astype(F32)
+    halves = [jnp.where(line_f + 128.0 * h == seat, 1.0, 0.0).astype(BF16) for h in range(2)]
+    sorter = jnp.concatenate(halves, axis=0)
+    sub = lax.broadcasted_iota(jnp.int32, (8, LOAD_PAD), 0)
+    facts = jnp.where(sub == 0, owner_f, jnp.where(sub == 1, mark_f, 0.0)).astype(BF16)
+    for quarter in range(NDP):
+        chosen = (line_f + 64.0 * quarter == seat) & (line < 64)
+        picked = jnp.where(chosen, 1.0, 0.0).astype(BF16)
+        meta_out[quarter] = dot(facts, picked, ((1,), (1,)))
+
+    await_bytes(raw_kv.at[rows, key_lanes], sem_in.at[0])
+    await_bytes(raw_kv.at[rows, value_lanes], sem_in.at[1])
+    for half in range(2):
+        moved = dot(sorter, raw_kv[:, half * 512:half * 512 + 512]).astype(BF16)
+        for head in range(KV_HEADS):
+            piece = moved[:, head * 128:head * 128 + 128]
+            sort_kv[:, 2 * head + half] = piece.reshape(NDP, 64, 128)
+
+    pl.semaphore_wait(barrier, len(peers))
+
+    here = dp * PLANE + j
+    for py, pj in plane[1:]:
+        remote(meta_out.at[py], meta_in.at[here], sem_as.at[0], sem_ar.at[0], z, pj, py)
+        remote(sort_kv.at[py, pj], xk.at[here], sem_as.at[1], sem_ar.at[1], z, pj, py)
+    local(meta_out.at[dp], meta_in.at[here], sem_ar.at[0])
+    local(sort_kv.at[dp, j], xk.at[here], sem_ar.at[1])
+
+    await_bytes(raw_q.at[rows, :], sem_in.at[2])
+    for jj in range(PLANE):
+        moved = dot(sorter, raw_q[:, jj * 256:jj * 256 + 256]).astype(BF16)
+        sort_q[:, jj] = moved.reshape(NDP, 64, 256)
+    for py, pj in plane[1:]:
+        remote(sort_q.at[py, pj], xq.at[here], sem_as.at[2], sem_ar.at[2], z, pj, py)
+    local(sort_q.at[dp, j], xq.at[here], sem_ar.at[2])
+
+    def grad_dst():
+        return gslab.at[pl.ds(pl.multiple_of(j * TOK, TOK), TOK), :]
+
+    def wide_column(pj):
+        return pl.ds(pl.multiple_of(pj * 256, 128), 256)
+
+    for d in range(1, PLANE):
+        pj = (j + d) % PLANE
+        remote(grad_ref.at[:, wide_column(pj)], grad_dst(), sem_as.at[3], sem_ar.at[3], z, pj)
+    local(grad_ref.at[:, wide_column(j)], grad_dst(), sem_ar.at[3])
+
+    def step_of(d):
+        return ((d + 1) // 2) * (2 * (d % 2) - 1)
+
+    def plane_of(d):
+        return (z + step_of(d) + NZ) % NZ
+
+    def source_of(d):
+        return (z - step_of(d) + NZ) % NZ
+
+    await_bytes(meta_in, sem_ar.at[0])
+    sources = NDP * PLANE
+    owners = meta_in[:, 0, :]
+    marks = meta_in[:, 1, :]
+    lane = lax.broadcasted_iota(jnp.int32, (sources, 128), 1)
+    source = lax.broadcasted_iota(jnp.int32, (sources, 128), 0)
+    used = lane < 64
+    owner_i = owners.astype(jnp.int32)
+    toward = jnp.where(used, owner_i >> 3, -1)
+    counts = jnp.zeros((sources, 128), F32)
+    for zz in range(NZ):
+        count = jnp.sum(jnp.where(toward == zz, 1.0, 0.0), axis=1, keepdims=True)
+        counts = jnp.where(lane == zz, count, counts)
+    earlier = jnp.where(
+        lax.broadcasted_iota(jnp.int32, (sources, sources), 1)
+        < lax.broadcasted_iota(jnp.int32, (sources, sources), 0), 1.0, 0.0).astype(BF16)
+    base = dot(earlier, counts.astype(BF16))
+    passed = jnp.zeros((sources, 1), F32)
+    lane_f = lane.astype(F32)
+    slot = jnp.full((sources, 128), -1.0, F32)
+    for zz in range(NZ):
+        order = lane_f + (base[:, zz:zz + 1] - passed)
+        passed = passed + counts[:, zz:zz + 1]
+        slot = jnp.where((toward == zz) & (order < CAP), order + zz * CAP, slot)
+    overflow = jnp.max(jnp.sum(counts, axis=0, keepdims=True), axis=1, keepdims=True)
+    overflow = jnp.where(overflow > CAP, 1.0, 0.0)
+    kind = ((source >> 3) * PLANE + (owner_i & (PLANE - 1))).astype(F32)
+
+    def paired(value):
+        turned = pltpu.roll(value, 64, 1)
+        first = lax.broadcasted_iota(jnp.int32, (1, 128), 1) < 64
+        return jnp.concatenate(
+            [jnp.where(first, value[2 * p:2 * p + 1], turned[2 * p + 1:2 * p + 2])
+             for p in range(sources // 2)], axis=1)
+
+    srow[...] = jnp.broadcast_to(paired(slot), (8, SLAB))
+    sub = lax.broadcasted_iota(jnp.int32, (8, SLAB), 0)
+    info[...] = jnp.where(sub == 0, paired(kind), jnp.where(sub == 1, paired(marks), 1.0)).astype(BF16)
+
+    await_bytes(xk, sem_ar.at[1])
+
+    def pack_first(zp):
+        row = (lax.broadcasted_iota(jnp.int32, (CAP, SLAB), 0) + zp * CAP).astype(F32)
+        hot = jnp.where(row == srow[0:1, :], 1.0, 0.0).astype(BF16)
+        onehot[zp] = hot
+        zs[0, zp] = dot(hot, xk[...].reshape(SLAB, 128)).astype(BF16)
+
+    landed = pl.ds(0, CAP)
+
+    @pl.loop(1, NZ)
+    def _(d):
+        zp = plane_of(d)
+        pack_first(zp)
+        remote(zs.at[0, zp], zr.at[0, z, landed, :], sem_zs.at[0], sem_zr.at[0], zp, j)
+
+    pack_first(z)
+    local(zs.at[0, z], zr.at[0, z, landed, :], sem_zr.at[0])
+
+    zr[:, :, CAP:, :] = jnp.zeros((3, NZ, 256 - CAP, 128), BF16)
+    sub8 = lax.broadcasted_iota(jnp.int32, (8, CAP), 0)
+
+    @pl.loop(0, NZ)
+    def _(d):
+        zp = plane_of(d)
+        ms[zp] = jnp.zeros((8, 256), F32)
+        told = dot(info[...], onehot[zp], ((1,), (1,)))
+        ms[zp, :, 0:CAP] = jnp.where(sub8 == 7, overflow, told)
+
+    for d in range(1, NZ):
+        zp = plane_of(d)
+        remote(ms.at[zp], mr.at[z], sem_zs.at[1], sem_zr.at[1], zp, j)
+    local(ms.at[z], mr.at[z], sem_zr.at[1])
+
+    await_bytes(xq, sem_ar.at[2])
+
+    @pl.loop(0, NZ)
+    def _(d):
+        zp = plane_of(d)
+        packed = dot(onehot[zp], xq[...].reshape(SLAB, 256))
+        zs[1, zp] = packed[:, :128].astype(BF16)
+        zs[2, zp] = packed[:, 128:].astype(BF16)
+
+    for d in range(1, NZ):
+        zp = plane_of(d)
+        remote(zs.at[1, zp], zr.at[1, z, landed, :], sem_zs.at[2], sem_zr.at[2], zp, j)
+    local(zs.at[1, z], zr.at[1, z, landed, :], sem_zr.at[2])
+
+    lengths = jnp.broadcast_to(len_ref[...].astype(F32), (DOCS, DOCS))
+    doc_row = lax.broadcasted_iota(jnp.int32, (DOCS, DOCS), 0)
+    doc_col = lax.broadcasted_iota(jnp.int32, (DOCS, DOCS), 1)
+    doc_ends = jnp.sum(jnp.where(doc_col <= doc_row, lengths, 0.0), axis=1, keepdims=True)
+    doc_size = jnp.sum(jnp.where(doc_col == doc_row, lengths, 0.0), axis=1, keepdims=True)
+    offset = lax.broadcasted_iota(jnp.int32, (1, TOK), 1)
+    for b in range(PLANE):
+        place_at = (offset + (z * SLAB + b * TOK)).astype(F32)
+        start = jnp.sum(jnp.where(doc_ends <= place_at, doc_size, 0.0), axis=0, keepdims=True)
+        low[b] = start.astype(jnp.int32) - (z * SLAB + b * TOK - HALO)
+    acc[...] = jnp.zeros_like(acc)
+
+    await_bytes(mr, sem_zr.at[1])
+    flag = mr[0, 7:8, 0:128]
+    for zz in range(1, NZ):
+        flag = jnp.maximum(flag, mr[zz, 7:8, 0:128])
+    flag_ref[...] = jnp.broadcast_to(flag, (8, 128)).astype(jnp.int32)
+    upper = jnp.where(
+        lax.broadcasted_iota(jnp.int32, (256, 256), 0)
+        < lax.broadcasted_iota(jnp.int32, (256, 256), 1), 1.0, 0.0).astype(BF16)
+    class_id = lax.broadcasted_iota(jnp.int32, (sources, 256), 0).astype(F32)
+    seen = jnp.zeros((sources, 1), F32)
+    for zz in range(NZ):
+        valid = mr[zz, 2:3, :] > 0.5
+        mine = (class_id == mr[zz, 0:1, :]) & valid
+        mine_f = jnp.where(mine, 1.0, 0.0)
+        order = dot(mine_f.astype(BF16), upper) + seen
+        seen = seen + jnp.sum(mine_f, axis=1, keepdims=True)
+        spot = jnp.sum(jnp.where(mine, order + class_id * 64.0, 0.0), axis=0, keepdims=True)
+        drow[zz] = jnp.broadcast_to(jnp.where(valid, spot, -1.0), (8, 256))
+    whole[...] = jnp.zeros_like(whole)
+
+    @pl.loop(0, NDP)
+    def _(w):
+        line = (lax.broadcasted_iota(jnp.int32, (512, 256), 0) + w * 512).astype(F32)
+        total = jnp.zeros((8, 512), F32)
+        for zz in range(NZ):
+            hot = jnp.where(line == drow[zz, 0:1, :], 1.0, 0.0).astype(BF16)
+            spread[zz, pl.ds(pl.multiple_of(w * 512, 512), 512), :] = hot
+            total = total + dot(mr[zz].astype(BF16), hot, ((1,), (1,)))
+        ym_out[w] = total
+
+    for e in range(1, NDP):
+        w = (dp + e) % NDP
+        remote(ym_out.at[w], ym_in.at[dp], sem_ys.at[0], sem_yr.at[0], z, j, w)
+    local(ym_out.at[dp], ym_in.at[dp], sem_yr.at[0])
+
+    def gather_all(chunk):
+        @pl.loop(0, NDP)
+        def _(w):
+            block = pl.ds(pl.multiple_of(w * 512, 512), 512)
+            total = jnp.zeros((512, 128), F32)
+            for zz in range(NZ):
+                total = total + dot(spread[zz, block, :], zr[chunk, zz])
+            ys[chunk, w] = total.astype(BF16).reshape(PLANE, 64, 128)
+
+    def send_back(chunk):
+        for e in range(1, NDP):
+            w = (dp + e) % NDP
+            remote(ys.at[chunk, w], yr.at[chunk, :, dp], sem_ys.at[1 + chunk], sem_yr.at[1 + chunk], z, j, w)
+        local(ys.at[chunk, dp], yr.at[chunk, :, dp], sem_yr.at[1 + chunk])
+
+    await_bytes(zr.at[0, :, landed, :], sem_zr.at[0])
+    gather_all(0)
+    send_back(0)
+
+    await_bytes(ym_in, sem_yr.at[0])
+    first = lax.broadcasted_iota(jnp.int32, (1, 128), 1) < 64
+    point = lax.broadcasted_iota(jnp.int32, (TOK, TOK), 0).astype(F32) + 1.0
+    for o in range(PLANE):
+        tile = slice(128 * (o // 2), 128 * (o // 2) + 128)
+        parts = [ym_in[e, 0:8, tile][1:2] for e in range(NDP)]
+        turned = [pltpu.roll(ym_in[e, 0:8, tile], 64, 1)[1:2] for e in range(NDP)]
+        left = parts if o % 2 == 0 else turned
+        right = turned if o % 2 == 0 else parts
+        mark = jnp.concatenate(
+            [jnp.where(first, left[0], right[1]), jnp.where(first, left[2], right[3])], axis=1)
+        place[o] = jnp.where(point == mark, 1.0, 0.0).astype(BF16)
+
+    def settle(chunk, o):
+        return dot(place[o], yr[chunk, o].reshape(TOK, 128)).astype(BF16)
+
+    await_bytes(yr.at[0], sem_yr.at[1])
+
+    @pl.loop(0, PLANE)
+    def _(o):
+        kv[c, pl.ds(pl.multiple_of(HALO + o * TOK, TOK), TOK), :] = settle(0, o)
+
+    own_kv = kv.at[c, pl.ds(HALO, SLAB), :]
+    remote(own_kv, own_kv, sem_es.at[0], sem_er.at[0], z, other)
+    tail = kv.at[c, pl.ds(SLAB, HALO), :]
+    head = kv.at[c, pl.ds(0, HALO), :]
+    remote(tail, head, sem_es.at[1], sem_er.at[1], up, j)
+    remote(tail, head, sem_es.at[1], sem_er.at[1], up, other)
+
+    for d in range(NZ):
+        zp = plane_of(d)
+        if d == 0:
+            local(zs.at[2, zp], zr.at[2, z, landed, :], sem_zr.at[3])
+        else:
+            remote(zs.at[2, zp], zr.at[2, z, landed, :], sem_zs.at[3], sem_zr.at[3 + d // 4], zp, j)
+
+    await_bytes(own_kv, sem_er.at[0])
+    await_bytes(kv.at[:, pl.ds(0, HALO), :], sem_er.at[1])
+    await_bytes(gslab, sem_ar.at[3])
+
+    def attend(head_index, b):
+        start = b * TOK if isinstance(b, int) else pl.multiple_of(b * TOK, TOK)
+        window = pl.ds(start, HALO + TOK)
+        query = settle(1 + head_index, b)
+        grad = gslab[pl.ds(start, TOK), head_index * 128:head_index * 128 + 128]
+        keys = kv[0, window, :]
+        values = kv[1, window, :]
+        key_index = lax.broadcasted_iota(jnp.int32, (HALO + TOK, TOK), 0)
+        query_index = lax.broadcasted_iota(jnp.int32, (HALO + TOK, TOK), 1)
+        allowed = (key_index >= low[b]) & (key_index <= query_index + HALO)
+        score = dot(keys, query, ((1,), (1,)))
+        score = jnp.where(allowed, score, MASKED)
+        top = jnp.max(score, axis=0, keepdims=True)
+        weights = jnp.exp((score - top) * SCALE)
+        weights = weights * (1.0 / jnp.sum(weights, axis=0, keepdims=True))
+        grad_weights = dot(values, grad, ((1,), (1,)))
+        row_dot = jnp.sum(weights * grad_weights, axis=0, keepdims=True)
+        grad_score = (weights * (grad_weights - row_dot)).astype(BF16)
+        acc[1, window, :] += dot(weights.astype(BF16), grad)
+        acc[0, window, :] += dot(grad_score, query) * SCALE
+        dqs[head_index, b] = (dot(grad_score, keys, ((0,), (0,))) * SCALE).astype(BF16)
+        column = pl.ds(pl.multiple_of(j * 256 + head_index * 128, 128), 128)
+
+        @pl.when(j == b)
+        def _():
+            local(dqs.at[head_index, b], dq_ref.at[:, column], sem_er.at[2])
+
+        @pl.when(j != b)
+        def _():
+            remote(dqs.at[head_index, b], dq_ref.at[:, column], sem_es.at[2], sem_er.at[2], z, b)
+
+    def hand_over(t):
+        ps[t] = acc[1 - c, HALO + t * TOK:HALO + t * TOK + TOK, :].astype(BF16)
+        remote(ps.at[t], pr.at[t], sem_es.at[4], sem_pr.at[t], z, other)
+
+    def finish(t):
+        await_bytes(pr.at[t], sem_pr.at[t])
+        total = acc[c, HALO + t * TOK:HALO + t * TOK + TOK, :] + pr[t].astype(F32)
+        outs[t] = total.astype(BF16)
+        column = pl.ds(pl.multiple_of(x * 128, 128), 128)
+        for which, ref in ((0, dk_ref), (1, dv_ref)):
+            @pl.when((c == which) & (j == t))
+            def _():
+                local(outs.at[t], ref.at[:, column], sem_er.at[4 + which])
+
+            @pl.when((c == which) & (j != t))
+            def _():
+                remote(outs.at[t], ref.at[:, column], sem_es.at[5], sem_er.at[4 + which], z, t)
+
+    await_bytes(zr.at[1, :, landed, :], sem_zr.at[2])
+    gather_all(1)
+    send_back(1)
+    await_bytes(yr.at[1], sem_yr.at[2])
+
+    @pl.loop(0, PLANE)
+    def _(b):
+        attend(0, b)
+
+    for group in range(4):
+        await_bytes(zr.at[2, pl.ds(0, 4), landed, :], sem_zr.at[3 + group])
+
+        @pl.loop(0, NDP)
+        def _(w):
+            block = pl.ds(pl.multiple_of(w * 512, 512), 512)
+            total = whole[block, :]
+            for d in range(4 * group, 4 * group + 4):
+                zz = source_of(d)
+                total = total + dot(spread[zz, block, :], zr[2, zz])
+            if group < 3:
+                whole[block, :] = total
+            else:
+                ys[2, w] = total.astype(BF16).reshape(PLANE, 64, 128)
+
+    for part in range(4):
+        pair = pl.ds(2 * part, 2)
+        for e in range(1, NDP):
+            w = (dp + e) % NDP
+            remote(ys.at[2, w, pair], yr.at[2, pair, dp], sem_ys.at[3], sem_yr.at[3 + part], z, j, w)
+        local(ys.at[2, dp, pair], yr.at[2, pair, dp], sem_yr.at[3 + part])
+
+    for b in range(PLANE):
+        if b == PLANE - 1:
+            await_bytes(hr, sem_er.at[3])
+            acc[:, SLAB:, :] += hr[...].astype(F32)
+        if b % 2 == 0:
+            await_bytes(yr.at[2, pl.ds(b, 2)], sem_yr.at[3 + b // 2])
+        attend(1, b)
+        if b == 1:
+            hs[...] = acc[:, :HALO, :].astype(BF16)
+            remote(hs, hr, sem_es.at[3], sem_er.at[3], down, j)
+        if b >= 2:
+            hand_over(b - 2)
+        if b >= 3:
+            finish(b - 3)
+    hand_over(6)
+    hand_over(7)
+    for t in (5, 6, 7):
+        finish(t)
+
+    seven = pl.ds(0, PLANE - 1)
+    most = pl.ds(0, NZ - 1)
+    many = pl.ds(0, NDP * PLANE - 1)
+    three = pl.ds(0, NDP - 1)
+    await_bytes(meta_in.at[many], sem_as.at[0])
+    await_bytes(xk.at[many], sem_as.at[1])
+    await_bytes(xq.at[many], sem_as.at[2])
+    await_bytes(gslab.at[pl.ds(0, 7 * TOK), :], sem_as.at[3])
+    await_bytes(zs.at[0, most], sem_zs.at[0])
+    await_bytes(ms.at[most], sem_zs.at[1])
+    await_bytes(zs.at[1, most], sem_zs.at[2])
+    await_bytes(zs.at[2, most], sem_zs.at[3])
+    await_bytes(ym_out.at[three], sem_ys.at[0])
+    for chunk in range(3):
+        await_bytes(ys.at[chunk, three], sem_ys.at[1 + chunk])
+    await_bytes(own_kv, sem_es.at[0])
+    await_bytes(kv.at[:, pl.ds(0, HALO), :], sem_es.at[1])
+    await_bytes(dqs.at[:, seven], sem_es.at[2])
+    await_bytes(hs, sem_es.at[3])
+    await_bytes(ps, sem_es.at[4])
+    await_bytes(outs.at[seven], sem_es.at[5])
+    await_bytes(dq_ref, sem_er.at[2])
+    await_bytes(dk_ref, sem_er.at[4])
+    await_bytes(dv_ref, sem_er.at[5])
+
+
+OUT_SHAPES = (
+    jax.ShapeDtypeStruct((TOK, HEADS * HEAD_DIM), BF16),
+    jax.ShapeDtypeStruct((TOK, KV_HEADS * HEAD_DIM), BF16),
+    jax.ShapeDtypeStruct((TOK, KV_HEADS * HEAD_DIM), BF16),
+)
+
+
+def spread_call(queries, key_rows, value_rows, slab_row, doc_lengths, out_grad):
     me = lax.axis_index("ctx")
     z = me // PLANE
     j = me % PLANE
@@ -311,7 +753,7 @@
     any_spec = pl.BlockSpec(memory_space=pl.ANY)
     vmem_spec = pl.BlockSpec(memory_space=pltpu.VMEM)
     dq, dkv = pl.pallas_call(
-        kernel,
+        spread_kernel,
         out_shape=(
             jax.ShapeDtypeStruct((TOK, HEADS * HEAD_DIM), BF16),
             jax.ShapeDtypeStruct((2, TOK, KV_HEADS * HEAD_DIM), BF16),
@@ -345,11 +787,72 @@
             pltpu.SemaphoreType.DMA((6,)),
         ],
         compiler_params=pltpu.CompilerParams(
-            collective_id=0, has_side_effects=True, vmem_limit_bytes=60 * 1024 * 1024
+            collective_id=1, has_side_effects=True, vmem_limit_bytes=60 * 1024 * 1024
         ),
-        name="packed_attention",
+        name="spread_attention",
     )(queries, key_rows, value_rows, slot, pos, out_grad, low)
     return (dq, dkv[0], dkv[1])
+
+
+def mixed_call(queries, key_rows, value_rows, out_grad, slab, doc_lengths):
+    any_spec = pl.BlockSpec(memory_space=pl.ANY)
+    vmem_spec = pl.BlockSpec(memory_space=pltpu.VMEM)
+    dma = pltpu.SemaphoreType.DMA
+    return pl.pallas_call(
+        mixed_kernel,
+        out_shape=OUT_SHAPES + (jax.ShapeDtypeStruct((8, 128), jnp.int32),),
+        in_specs=[any_spec] * 4 + [vmem_spec] * 2,
+        out_specs=(any_spec, any_spec, any_spec, vmem_spec),
+        scratch_shapes=[
+            pltpu.VMEM((PLANE, 1, TOK), jnp.int32),
+            pltpu.VMEM((LOAD_PAD, 1024), BF16),
+            pltpu.VMEM((LOAD_PAD, 2048), BF16),
+            pltpu.VMEM((NDP, PLANE, 64, 128), BF16),
+            pltpu.VMEM((NDP, PLANE, 64, 256), BF16),
+            pltpu.VMEM((NDP, 8, 128), F32),
+            pltpu.VMEM((NDP * PLANE, 8, 128), F32),
+            pltpu.VMEM((NDP * PLANE, 64, 128), BF16),
+            pltpu.VMEM((NDP * PLANE, 64, 256), BF16),
+            pltpu.VMEM((8, SLAB), F32),
+            pltpu.VMEM((8, SLAB), BF16),
+            pltpu.VMEM((SLAB, 256), BF16),
+            pltpu.VMEM((NZ, CAP, SLAB), BF16),
+            pltpu.VMEM((3, NZ, CAP, 128), BF16),
+            pltpu.VMEM((NZ, 8, 256), F32),
+            pltpu.VMEM((3, NZ, 256, 128), BF16),
+            pltpu.VMEM((NZ, 8, 256), F32),
+            pltpu.VMEM((NZ, 8, 256), F32),
+            pltpu.VMEM((NZ, SLAB, 256), BF16),
+            pltpu.VMEM((SLAB, 128), F32),
+            pltpu.VMEM((3, NDP, PLANE, 64, 128), BF16),
+            pltpu.VMEM((3, PLANE, NDP, 64, 128), BF16),
+            pltpu.VMEM((NDP, 8, 512), F32),
+            pltpu.VMEM((NDP, 8, 512), F32),
+            pltpu.VMEM((PLANE, TOK, TOK), BF16),
+            pltpu.VMEM((2, HALO + SLAB, 128), BF16),
+            pltpu.VMEM((2, HALO + SLAB, 128), F32),
+            pltpu.VMEM((2, PLANE, TOK, 128), BF16),
+            pltpu.VMEM((2, HALO, 128), BF16),
+            pltpu.VMEM((2, HALO, 128), BF16),
+            pltpu.VMEM((PLANE, TOK, 128), BF16),
+            pltpu.VMEM((PLANE, TOK, 128), BF16),
+            pltpu.VMEM((PLANE, TOK, 128), BF16),
+            dma((3,)), dma((4,)), dma((4,)), dma((4,)), dma((7,)), dma((4,)), dma((7,)),
+            dma((6,)), dma((6,)), dma((8,)),
+        ],
+        compiler_params=pltpu.CompilerParams(
+            collective_id=0, has_side_effects=True, vmem_limit_bytes=62 * 1024 * 1024
+        ),
+        name="mixed_attention",
+    )(queries, key_rows, value_rows, out_grad, slab, doc_lengths)
+
+
+def body(queries, key_rows, value_rows, slab_row, doc_lengths, out_grad):
+    slab = jnp.pad(slab_row, (0, LOAD_PAD - LOAD), constant_values=-1)
+    slab = jnp.broadcast_to(slab[None, :], (8, LOAD_PAD))
+    operands = (queries, key_rows, value_rows, slab_row, doc_lengths, out_grad)
+    dq, dk, dv, flag = mixed_call(queries, key_rows, value_rows, out_grad, slab, doc_lengths)
+    return lax.cond(flag[0, 0] > 0, lambda: tuple(spread_call(*operands)), lambda: (dq, dk, dv))
 
 
 def solution(mesh):

time: 200 us -> 174 us (0.87)
  Pallas kernels: 191 us -> 167 us
  other arithmetic: 4.05 us -> 0 us
    pallas_call x1, Pallas kernels: 191 us -> 167 us  [mixed_call(): pl.pallas_call(mixed_kernel, out_shape=OUT_SHAPES + (jax.ShapeDtypeStruct...]
    unnamed x3 -> x11, local copies, waits for them, and re-layouts: 0.97 us -> 3.77 us
where the time goes in v2:
time: 174 us
  Pallas kernels  167 us (96%)
  local copies, waits for them, and re-layouts  6.24 us (4%)
    pallas_call x1, Pallas kernels, mixed_call(): pl.pallas_call(mixed_kernel, out_shape=OUT_SHAPES + (jax.ShapeDtypeStruct...  167 us
    unnamed x11, local copies, waits for them, and re-layouts  3.77 us

profile of v2, /device:TPU:1, one launch (start us, length us, event | category | flops | bytes accessed | tf_op | source)
XLA Modules:
  0.0 174.1 jit_solution(14455081834989162584)
XLA Ops:
  0.6 0.7 pad.7
  1.3 0.6 broadcast_in_dim.30.slab_ref
  1.9 0.0 copy-start
  1.9 0.0 copy-start.1
  1.9 0.0 copy-start.2
  1.9 166.5 %mixed_attention.1 = (bf16[256,2048]{1,0:T(8,128)(2,1)}, bf16[256,512]{1,0:T(8,128)(2,1)S(1)}, bf16[256,512]{1,0:T(8,128)(2,1)}, s32[8,128]{1,0:T(8,128)}) custom-call(bf16[288,2048]{1,0:T(8,128)(2,1)} %q_ref.1, bf16[288,512]{1,0:T(8,128)(2,1)} %k_ref.1, bf16[288,512]{1,0:T(8,128)(2,1)} %v_ref.1, bf16[256,2048]{1,0:T(8,128)(2,1)} %grad_ref.1, ...), custom_call_target="tpu_custom_call" | custom-call | tf_op jit(solution)/shard_map/mixed_attention/pallas_call | solution.py:801
  168.5 1.2 slice.9
  170.3 0.0 copy-done
  170.3 0.0 copy-done.1
  170.3 0.0 copy-done.2
  170.4 0.0 copy-start.3
  170.4 2.3 %copy.27 = bf16[256,2048]{1,0:T(8,128)(2,1)} copy(bf16[256,2048]{1,0:T(8,128)(2,1)} %get-tuple-element.57) | data formatting | bytes 2097152
  172.7 0.7 copy.28
  173.4 0.0 copy-done.3
  173.4 0.7 copy.29
  (1 shorter events, 0.0 us)
Async XLA Ops:
  1.9 168.4 %copy-start = (bf16[288,2048]{1,0:T(8,128)(2,1)S(1)}, bf16[288,2048]{1,0:T(8,128)(2,1)}, u32[]{:S(2)}) copy-start(bf16[288,2048]{1,0:T(8,128)(2,1)} %q_ref.1) | copy-start | bytes 3538948
  1.9 168.4 %copy-start.1 = (bf16[288,512]{1,0:T(8,128)(2,1)S(1)}, bf16[288,512]{1,0:T(8,128)(2,1)}, u32[]{:S(2)}) copy-start(bf16[288,512]{1,0:T(8,128)(2,1)} %k_ref.1) | copy-start | bytes 884740
  1.9 168.4 %copy-start.2 = (bf16[288,512]{1,0:T(8,128)(2,1)S(1)}, bf16[288,512]{1,0:T(8,128)(2,1)}, u32[]{:S(2)}) copy-start(bf16[288,512]{1,0:T(8,128)(2,1)} %v_ref.1) | copy-start | bytes 884740
  170.4 3.1 %copy-start.3 = (bf16[256,512]{1,0:T(8,128)(2,1)S(1)}, bf16[256,512]{1,0:T(8,128)(2,1)}, u32[]{:S(2)}) copy-start(bf16[256,512]{1,0:T(8,128)(2,1)} %get-tuple-element.59) | copy-start | bytes 786436
